TPU v7x, 32 devices: a whole 2x2x4 slice. The times are simulated.
32 devices in a mesh: segment: 4 (over y, x), tok: 8 (over z, core).
Axes of the slice: x: 2, y: 2, z: 4, core: 2. Of those that a mesh axis runs over, the one named last changes fastest.
Arguments:
- inputs: bfloat16 [2, 16, 8192], P(None, 'tok'), may hold values from -6 to 6
- weights: bfloat16 [4, 8192, 8192], P('segment', None, 'tok'), may hold values from -0.09375 to 0.09375
- keep_mask: int32 [4, 64, 64], P('segment', None, 'tok'), may hold values 0 or 1
- gains: float32 [4, 8192], P('segment'), may hold values from 0.1 to 1.9
Outputs:
- acts: bfloat16 [4, 2, 16, 8192], P('segment', None, 'tok')
- factors: float32 [4, 1024, 1024], P('segment')
All inputs are finite; a program needn't handle non-finite values. No bound on the sum of `keep_mask` on one device may be relied on, other than what follows from the above.
Results may differ from a plain program's by a relative error of at most 0.0072.
Values may be sent and summed in bfloat16 or wider, within the bound.
A program may use at most 128 MiB of HBM per device.

v0:
```python
import jax
import jax.numpy as jnp
from jax import lax
from jax.sharding import PartitionSpec as P

GRP = 1024


norm_eps = 1e-05
damp_share = 0.25


def shifted(value, axis, by):
    devices = lax.axis_size(axis)
    pairs = [(i, i + by) for i in range(devices) if 0 <= i + by < devices]
    return lax.ppermute(value, axis, pairs)


def local(inputs, weights, keep_mask, gains):
    segment_count = lax.axis_size("segment")
    segment_idx = lax.axis_index("segment")
    tok_count = lax.axis_size("tok")
    tok_idx = lax.axis_index("tok")
    micro_count, row_count, width = inputs.shape
    col_width = weights.shape[2]
    nblk = keep_mask.shape[1]
    blk_size = width // nblk
    col_blocks = keep_mask.shape[2]
    block_mask = keep_mask[0].astype(jnp.bfloat16)
    pruned = (
        weights[0].reshape(nblk, blk_size, col_blocks, blk_size) * block_mask[:, None, :, None]
    ).reshape(width, col_width)
    gain_row = gains[0][None, :]
    col_start = tok_idx * col_width
    gram = jnp.zeros((GRP, GRP), jnp.float32)
    tick_total = micro_count + segment_count - 1
    received = jnp.zeros((row_count, width), jnp.bfloat16)
    stored = jnp.zeros((micro_count, row_count, width), jnp.bfloat16)
    for tick_num in range(tick_total):
        micro_now = tick_num - segment_idx
        valid = jnp.logical_and(micro_now >= 0, micro_now < micro_count)
        current = jnp.where(segment_idx == 0, inputs[min(tick_num, micro_count - 1)], received)
        group_cols = current[:, :GRP]
        gram = gram + jnp.where(
            valid,
            lax.dot_general(
                group_cols, group_cols, (((0,), (0,)), ((), ())), preferred_element_type=jnp.float32
            ),
            0.0,
        )
        row_vals = lax.all_gather(current, "tok", axis=0, tiled=True).astype(jnp.float32)
        mean_sq = jnp.mean(row_vals * row_vals, axis=-1, keepdims=True)
        normed = (row_vals * lax.rsqrt(mean_sq + norm_eps) * gain_row).astype(jnp.bfloat16)
        product = jnp.dot(normed, pruned, preferred_element_type=jnp.float32)
        resid_cols = lax.dynamic_slice_in_dim(row_vals, col_start, col_width, 1)
        new_cols = (resid_cols + product).astype(jnp.bfloat16)
        output = lax.all_to_all(new_cols, "tok", split_axis=0, concat_axis=1, tiled=True)
        slot = jnp.clip(micro_now, 0, micro_count - 1)
        stored = jnp.where(valid, lax.dynamic_update_index_in_dim(stored, output, slot, 0), stored)
        received = shifted(output, "segment", 1)
    total = lax.psum(gram, "tok")
    hess = total / (micro_count * row_count * tok_count)
    damp_val = damp_share * jnp.mean(jnp.diagonal(hess))
    hess = hess + damp_val * jnp.eye(GRP, dtype=jnp.float32)
    factor = jnp.linalg.cholesky(hess).T
    return (stored[None], factor[None])


def solution(mesh):
    return jax.shard_map(
        local,
        mesh=mesh,
        in_specs=(
            P(None, "tok", None),
            P("segment", None, "tok"),
            P("segment", None, "tok"),
            P("segment", None),
        ),
        out_specs=(P("segment", None, "tok", None), P("segment", None, None)),
        check_vma=False,
    )
```

profile of v0, /device:TPU:7, one launch (start us, length us, event | category | flops | bytes accessed | tf_op | source)
XLA Modules:
  0.0 571.1 jit_solution(9112144295885902198)
XLA Ops:
  8.0 15.5 %all-gather = bf16[1,16,8192]{2,0,1:T(2,128)(2,1)S(1)} all-gather(bf16[1,2,8192]{2,0,1:T(2,128)(2,1)S(1)} %broadcast_select_fusion), channel_id=2, replica_groups=mesh['segment'=4,'tok'=8] {'tok'}, dimensions={1}, use_global_device_ids=true | all-gather | bytes 294912 | tf_op jit(solution)/shard_map/all_gather | solution.py:51
  25.1 2.8 mul.116
  27.9 2.9 copy-done
  30.9 6.0 %bitcast_multiply_fusion = bf16[8192,1024]{1,0:T(8,128)(2,1)} fusion(bf16[1024,8,8,128]{3,2,1,0:T(8,128)(2,1)S(1)} %bitcast.112, bf16[1,8192,1024]{2,1,0:T(8,128)(2,1)S(1)} %copy-done), kind=kLoop, calls=%fused_computation.1 | loop fusion | flops 8388608 | bytes 50331648 | tf_op jit(solution)/shard_map/mul | solution.py:31
  36.9 8.1 %fusion.1 = bf16[16,1024]{1,0:T(8,128)(2,1)S(1)} fusion(bf16[8192,1024]{1,0:T(8,128)(2,1)} %bitcast_multiply_fusion, f32[1,16,8192]{2,1,0:T(8,128)S(1)} %copy_convert_fusion, f32[8192]{0:T(1024)S(1)} %bitcast.113, f32[16]{0:T(128)S(1)} %add_rsqrt_fusion.4, s32[]{:T(128)S(6)} %select_n.140), kind=kOutput, calls=%fused_computation.28 | convolution fusion | flops 268861440 | bytes 17433092 | tf_op jit(solution)/shard_map/dot_general | solution.py:54
  45.6 4.9 all-to-all-start
  50.6 2.7 fusion.59
  53.3 2.2 all-to-all-done
  55.5 1.3 collective-permute-start
  56.8 3.3 collective-permute-done
  60.2 15.9 %all-gather.1 = bf16[8,2,8192]{2,1,0:T(2,128)(2,1)S(1)} all-gather(bf16[1,2,8192]{2,1,0:T(2,128)(2,1)S(1)} %bitcast.119), channel_id=1, replica_groups=mesh['segment'=4,'tok'=8] {'tok'}, dimensions={0}, use_global_device_ids=true | all-gather | bytes 294912 | tf_op jit(solution)/shard_map/all_gather | solution.py:51
  76.4 8.1 %fusion.2 = bf16[16,1024]{1,0:T(8,128)(2,1)S(1)} fusion(bf16[8192,1024]{1,0:T(8,128)(2,1)} %bitcast_multiply_fusion, f32[16,8192]{1,0:T(8,128)S(1)} %reshape.162, f32[16]{0:T(128)S(1)} %add_rsqrt_fusion.3, f32[8192]{0:T(1024)S(1)} %bitcast.114, s32[]{:T(128)S(6)} %select_n.140), kind=kOutput, calls=%fused_computation.29 | convolution fusion | flops 268861440 | bytes 17433092 | tf_op jit(solution)/shard_map/dot_general | solution.py:54
  85.1 3.4 all-to-all-start.1
  88.6 4.9 all-to-all-done.1
  93.6 1.3 collective-permute-start.1
  94.8 2.7 fusion.57
  98.2 16.1 %all-gather.2 = bf16[8,2,8192]{2,1,0:T(2,128)(2,1)S(1)} all-gather(bf16[1,2,8192]{2,1,0:T(2,128)(2,1)S(1)} %bitcast.120), channel_id=1, replica_groups=mesh['segment'=4,'tok'=8] {'tok'}, dimensions={0}, use_global_device_ids=true | all-gather | bytes 294912 | tf_op jit(solution)/shard_map/all_gather | solution.py:51
  114.6 8.1 %fusion.3 = bf16[16,1024]{1,0:T(8,128)(2,1)S(1)} fusion(bf16[8192,1024]{1,0:T(8,128)(2,1)} %bitcast_multiply_fusion, f32[16,8192]{1,0:T(8,128)S(1)} %reshape.163, f32[16]{0:T(128)S(1)} %add_rsqrt_fusion.2, f32[8192]{0:T(1024)S(1)} %bitcast.115, s32[]{:T(128)S(6)} %select_n.140), kind=kOutput, calls=%fused_computation.30 | convolution fusion | flops 268861440 | bytes 17433092 | tf_op jit(solution)/shard_map/dot_general | solution.py:54
  123.4 3.4 all-to-all-start.2
  126.9 5.0 all-to-all-done.2
  133.1 2.7 fusion.55
  135.8 1.3 collective-permute-done.2
  137.1 15.7 %all-gather.3 = bf16[8,2,8192]{2,1,0:T(2,128)(2,1)S(1)} all-gather(bf16[1,2,8192]{2,1,0:T(2,128)(2,1)S(1)} %bitcast.121), channel_id=1, replica_groups=mesh['segment'=4,'tok'=8] {'tok'}, dimensions={0}, use_global_device_ids=true | all-gather | bytes 294912 | tf_op jit(solution)/shard_map/all_gather | solution.py:51
  153.0 8.1 %fusion.4 = bf16[16,1024]{1,0:T(8,128)(2,1)S(1)} fusion(bf16[8192,1024]{1,0:T(8,128)(2,1)} %bitcast_multiply_fusion, f32[16,8192]{1,0:T(8,128)S(1)} %reshape.164, f32[16]{0:T(128)S(1)} %add_rsqrt_fusion.1, f32[8192]{0:T(1024)S(1)} %bitcast.116, s32[]{:T(128)S(6)} %select_n.140), kind=kOutput, calls=%fused_computation.31 | convolution fusion | flops 268861440 | bytes 17433092 | tf_op jit(solution)/shard_map/dot_general | solution.py:54
  161.8 3.4 all-to-all-start.3
  165.3 5.0 all-to-all-done.3
  171.5 2.8 fusion.53
  174.3 1.8 collective-permute-done.3
  176.1 15.7 %all-gather.4 = bf16[8,2,8192]{2,1,0:T(2,128)(2,1)S(1)} all-gather(bf16[1,2,8192]{2,1,0:T(2,128)(2,1)S(1)} %bitcast.122), channel_id=1, replica_groups=mesh['segment'=4,'tok'=8] {'tok'}, dimensions={0}, use_global_device_ids=true | all-gather | bytes 294912 | tf_op jit(solution)/shard_map/all_gather | solution.py:51
  192.0 8.1 %fusion.5 = bf16[16,1024]{1,0:T(8,128)(2,1)S(1)} fusion(bf16[8192,1024]{1,0:T(8,128)(2,1)} %bitcast_multiply_fusion, f32[16,8192]{1,0:T(8,128)S(1)} %reshape.165, f32[16]{0:T(128)S(1)} %add_rsqrt_fusion, f32[8192]{0:T(1024)S(1)} %bitcast.117, s32[]{:T(128)S(6)} %select_n.140), kind=kOutput, calls=%fused_computation.32 | convolution fusion | flops 268861440 | bytes 17433092 | tf_op jit(solution)/shard_map/dot_general | solution.py:54
  200.8 3.4 all-to-all-start.4
  204.2 5.6 select_add_fusion.1
  210.0 99.7 %all-reduce.3.cloned.1.call-done = f32[1024,1024]{0,1:T(8,128)} async-done(((f32[1024,1024]{0,1:T(8,128)}), f32[1024,1024]{0,1:T(8,128)}) %all-reduce.3.cloned.1.call-update) | async-done | bytes 4194320 | tf_op jit(solution)/shard_map/psum | solution.py:61
  309.7 5.0 broadcast_multiply_fusion
  314.7 17.0 %gather_fusion = f32[1024]{0:T(1024)S(1)} fusion(f32[1024,1024]{0,1:T(8,128)} %broadcast_multiply_fusion, s32[1024]{0:T(1024)S(1)} %bitcast.111), kind=kCustom, calls=%fused_computation | custom fusion | bytes 16384 | tf_op jit(solution)/shard_map/jit(diagonal)/cond/branch_0_fun/gather | solution.py:63
  333.0 5.1 select_add_fusion
  338.1 5.7 %copy.82 = f32[1024,1024]{1,0:T(8,128)} copy(f32[1024,1024]{0,1:T(8,128)} %select_add_fusion) | data formatting | bytes 8388608 | tf_op jit(solution)/shard_map/add | solution.py:64
  343.8 4.5 fusion
  348.3 1.9 copy-done.1
  350.2 11.7 %cholesky.222 = f32[128,128]{1,0:T(8,128)S(1)} custom-call(f32[128,128]{1,0:T(8,128)S(1)} %cholesky.577), custom_call_target="Cholesky" | custom-call | tf_op jit(solution)/shard_map/jit(cholesky)/cholesky | solution.py:65
  362.1 9.8 %custom-call.59 = f32[1,128,128]{1,2,0:T(8,128)S(1)} custom-call(f32[1,128,128]{2,1,0:T(8,128)S(1)} %get-tuple-element.15), custom_call_target="InvertDiagBlocksLowerTriangular" | custom-call | tf_op jit(solution)/shard_map/jit(cholesky)/cholesky | solution.py:65
  371.9 1.5 fusion.15
  373.6 1.6 convolution_subtract_fusion
  375.2 11.7 %cholesky.243 = f32[128,128]{1,0:T(8,128)S(1)} custom-call(f32[128,128]{1,0:T(8,128)S(1)} %cholesky.581), custom_call_target="Cholesky" | custom-call | tf_op jit(solution)/shard_map/jit(cholesky)/cholesky | solution.py:65
  387.2 2.5 cholesky.254
  389.7 9.8 %custom-call.60 = f32[1,128,128]{1,2,0:T(8,128)S(1)} custom-call(f32[1,128,128]{2,1,0:T(8,128)S(1)} %get-tuple-element.13), custom_call_target="InvertDiagBlocksLowerTriangular" | custom-call | tf_op jit(solution)/shard_map/jit(cholesky)/cholesky | solution.py:65
  402.2 2.7 convolution_subtract_fusion.1
  405.0 11.7 %cholesky.466 = f32[128,128]{1,0:T(8,128)S(1)} custom-call(f32[128,128]{1,0:T(8,128)S(1)} %cholesky.586), custom_call_target="Cholesky" | custom-call | tf_op jit(solution)/shard_map/jit(cholesky)/cholesky | solution.py:65
  417.5 9.8 %custom-call.61 = f32[1,128,128]{1,2,0:T(8,128)S(1)} custom-call(f32[1,128,128]{2,1,0:T(8,128)S(1)} %get-tuple-element.11), custom_call_target="InvertDiagBlocksLowerTriangular" | custom-call | tf_op jit(solution)/shard_map/jit(cholesky)/cholesky | solution.py:65
  428.5 3.3 convolution_subtract_fusion.2
  431.8 11.7 %cholesky.485 = f32[128,128]{1,0:T(8,128)S(1)} custom-call(f32[128,128]{1,0:T(8,128)S(1)} %cholesky.591), custom_call_target="Cholesky" | custom-call | tf_op jit(solution)/shard_map/jit(cholesky)/cholesky | solution.py:65
  444.3 9.8 %custom-call.62 = f32[1,128,128]{1,2,0:T(8,128)S(1)} custom-call(f32[1,128,128]{2,1,0:T(8,128)S(1)} %get-tuple-element.9), custom_call_target="InvertDiagBlocksLowerTriangular" | custom-call | tf_op jit(solution)/shard_map/jit(cholesky)/cholesky | solution.py:65
  455.3 3.2 convolution_subtract_fusion.3
  458.5 12.1 %cholesky.504 = f32[128,128]{1,0:T(8,128)S(1)} custom-call(f32[128,128]{1,0:T(8,128)S(1)} %cholesky.596), custom_call_target="Cholesky" | custom-call | tf_op jit(solution)/shard_map/jit(cholesky)/cholesky | solution.py:65
  471.3 9.8 %custom-call.63 = f32[1,128,128]{1,2,0:T(8,128)S(1)} custom-call(f32[1,128,128]{2,1,0:T(8,128)S(1)} %get-tuple-element.7), custom_call_target="InvertDiagBlocksLowerTriangular" | custom-call | tf_op jit(solution)/shard_map/jit(cholesky)/cholesky | solution.py:65
  482.2 3.1 convolution_subtract_fusion.4
  485.3 11.7 %cholesky.524 = f32[128,128]{1,0:T(8,128)S(1)} custom-call(f32[128,128]{1,0:T(8,128)S(1)} %cholesky.601), custom_call_target="Cholesky" | custom-call | tf_op jit(solution)/shard_map/jit(cholesky)/cholesky | solution.py:65
  497.8 9.8 %custom-call.64 = f32[1,128,128]{1,2,0:T(8,128)S(1)} custom-call(f32[1,128,128]{2,1,0:T(8,128)S(1)} %get-tuple-element.5), custom_call_target="InvertDiagBlocksLowerTriangular" | custom-call | tf_op jit(solution)/shard_map/jit(cholesky)/cholesky | solution.py:65
  508.6 2.8 convolution_subtract_fusion.5
  511.5 11.7 %cholesky.544 = f32[128,128]{1,0:T(8,128)S(1)} custom-call(f32[128,128]{1,0:T(8,128)S(1)} %cholesky.606), custom_call_target="Cholesky" | custom-call | tf_op jit(solution)/shard_map/jit(cholesky)/cholesky | solution.py:65
  524.0 9.8 %custom-call.65 = f32[1,128,128]{1,2,0:T(8,128)S(1)} custom-call(f32[1,128,128]{2,1,0:T(8,128)S(1)} %get-tuple-element.3), custom_call_target="InvertDiagBlocksLowerTriangular" | custom-call | tf_op jit(solution)/shard_map/jit(cholesky)/cholesky | solution.py:65
  534.7 2.3 convolution_subtract_fusion.6
  537.0 11.7 %cholesky.562 = f32[128,128]{1,0:T(8,128)S(1)} custom-call(f32[128,128]{1,0:T(8,128)S(1)} %convolution_subtract_fusion.6), custom_call_target="Cholesky" | custom-call | tf_op jit(solution)/shard_map/jit(cholesky)/cholesky | solution.py:65
  559.2 4.9 select_bitcast_fusion
  (98 shorter events, 29.1 us)
Async XLA Ops:
  25.1 5.8 %copy-start = (bf16[1,8192,1024]{2,1,0:T(8,128)(2,1)S(1)}, bf16[1,8192,1024]{2,1,0:T(8,128)(2,1)}, u32[]{:S(2)}) copy-start(bf16[1,8192,1024]{2,1,0:T(8,128)(2,1)} %param.5) | copy-start | bytes 50331652
  30.9 6.1 %copy-start.2 = (f32[1,8192]{1,0:T(1,128)S(1)}, f32[1,8192]{1,0:T(1,128)}, u32[]{:S(2)}) copy-start(f32[1,8192]{1,0:T(1,128)} %param.7) | copy-start | bytes 98308
  45.0 15.1 %copy-start.3 = (bf16[2,2,8192]{2,1,0:T(2,128)(2,1)S(1)}, bf16[2,2,8192]{2,1,0:T(2,128)(2,1)}, u32[]{:S(2)}) copy-start(bf16[2,2,8192]{2,1,0:T(2,128)(2,1)} %param.4) | copy-start | bytes 196612
  45.6 9.8 %all-to-all-start = ((bf16[8,2,1024]{2,1,0:T(2,128)(2,1)}), bf16[8,2,1024]{2,1,0:T(2,128)(2,1)S(1)}, u32[]{:S(2)}, u32[]{:S(2)}) async-start(bf16[8,2,1024]{2,1,0:T(2,128)(2,1)} %all_to_all.68), calls=%async_computation | async-start | bytes 65536 | tf_op jit(solution)/shard_map/all_to_all | solution.py:57
  55.5 4.6 collective-permute-start
  85.1 8.4 %all-to-all-start.1 = ((bf16[8,2,1024]{2,1,0:T(2,128)(2,1)}), bf16[8,2,1024]{2,1,0:T(2,128)(2,1)S(1)}, u32[]{:S(2)}, u32[]{:S(2)}) async-start(bf16[8,2,1024]{2,1,0:T(2,128)(2,1)} %all_to_all.72), calls=%async_computation.1 | async-start | bytes 65536 | tf_op jit(solution)/shard_map/all_to_all | solution.py:57
  93.6 4.6 collective-permute-start.1
  123.4 8.4 %all-to-all-start.2 = ((bf16[8,2,1024]{2,1,0:T(2,128)(2,1)}), bf16[8,2,1024]{2,1,0:T(2,128)(2,1)S(1)}, u32[]{:S(2)}, u32[]{:S(2)}) async-start(bf16[8,2,1024]{2,1,0:T(2,128)(2,1)} %all_to_all.76), calls=%async_computation.2 | async-start | bytes 65536 | tf_op jit(solution)/shard_map/all_to_all | solution.py:57
  131.8 5.2 collective-permute-start.2
  161.8 8.4 %all-to-all-start.3 = ((bf16[8,2,1024]{2,1,0:T(2,128)(2,1)}), bf16[8,2,1024]{2,1,0:T(2,128)(2,1)S(1)}, u32[]{:S(2)}, u32[]{:S(2)}) async-start(bf16[8,2,1024]{2,1,0:T(2,128)(2,1)} %all_to_all.80), calls=%async_computation.3 | async-start | bytes 65536 | tf_op jit(solution)/shard_map/all_to_all | solution.py:57
  170.2 5.8 %collective-permute-start.3 = (bf16[2,8192]{1,0:T(2,128)(2,1)S(1)}, bf16[2,8192]{1,0:T(2,128)(2,1)S(1)}, u32[]{:S(2)}, u32[]{:S(2)}) collective-permute-start(bf16[2,8192]{1,0:T(2,128)(2,1)S(1)} %bitcast.123), channel_id=1, source_target_pairs={{0,8},{8,16},{16,24},{1,9},{9,17},{17,25},{2,10},{10,18},{18,26},{... | collective-permute-start | bytes 98312 | tf_op jit(solution)/shard_map/ppermute | solution.py:16
  200.8 9.1 %all-to-all-start.4 = ((bf16[8,2,1024]{2,1,0:T(2,128)(2,1)}), bf16[8,2,1024]{2,1,0:T(2,128)(2,1)S(1)}, u32[]{:S(2)}, u32[]{:S(2)}) async-start(bf16[8,2,1024]{2,1,0:T(2,128)(2,1)} %all_to_all.84), calls=%async_computation.4 | async-start | bytes 65536 | tf_op jit(solution)/shard_map/all_to_all | solution.py:57
  204.2 105.5 %all-reduce.3.cloned.1.call-start = ((), (), s32[]{:S(2)}) async-start(), calls=%async_computation.5 | async-start | bytes 8388608 | tf_op jit(solution)/shard_map/psum | solution.py:61
  210.0 104.7 %copy-start.4 = (bf16[1,2,2,8192]{3,2,1,0:T(2,128)(2,1)}, bf16[1,2,2,8192]{3,2,1,0:T(2,128)(2,1)S(1)}, u32[]{:S(2)}) copy-start(bf16[1,2,2,8192]{3,2,1,0:T(2,128)(2,1)S(1)} %fusion.51) | copy-start | bytes 196612
  348.3 1.9 copy-start.1
Sparse Core Ops, SparseCore 0:
  209.9 99.7 all-reduce.2
where the time goes:
time: 582 us; the launch traced here: 571 us
  other arithmetic  196 us (34%)
  waiting for transfers between devices  124 us (21%)
  matrix products  84.1 us (14%)
  blocking collectives  79 us (14%)
  local copies, waits for them, and re-layouts  44 us (8%)
  starting transfers between devices  23.6 us (4%)
  between operations  20.3 us (3%)
    another operation x30, other arithmetic, local(): factor = jnp.linalg.cholesky(hess).T  168 us
    psum x1, waiting for transfers between devices, local(): total = lax.psum(gram, 'tok')  99.7 us
    all_gather x5, blocking collectives, local(): lax.all_gather(current, 'tok', axis=0, tiled=True).astype(jnp.float32)  79 us
    dot_general x5, matrix products, local(): product = jnp.dot(normed, pruned, preferred_element_type=jnp.float32)  40.5 us
    another operation x14, matrix products, local(): factor = jnp.linalg.cholesky(hess).T  27.1 us
    all_to_all x5, starting transfers between devices, local(): lax.all_to_all(new_cols, 'tok', split_axis=0, concat_axis=1, tiled=True)  18.5 us
    gather x1, local copies, waits for them, and re-layouts, local(): damp_val = damp_share * jnp.mean(jnp.diagonal(hess))  17 us
    all_to_all x5, waiting for transfers between devices, local(): lax.all_to_all(new_cols, 'tok', split_axis=0, concat_axis=1, tiled=True)  17 us
  transfers between devices with their start and end apart: 10, of which 9 were waited for; matrix products, arithmetic and copies ran while one was open for 3% of the time, Pallas kernels for 0%

commit v1 on v0

v1 whole, which is shorter than its diff:
```python
import functools

import jax
import jax.numpy as jnp
from jax import lax
from jax.experimental import pallas as pl
from jax.experimental.pallas import tpu as pltpu
from jax.sharding import PartitionSpec as P

GRP = 1024
LANES = 128
RANK_MAX = 64


norm_eps = 1e-05
damp_share = 0.25


def parts3(value):
    high = value.astype(jnp.bfloat16)
    rest = value - high.astype(jnp.float32)
    mid = rest.astype(jnp.bfloat16)
    low = (rest - mid.astype(jnp.float32)).astype(jnp.bfloat16)
    return jnp.concatenate([high, mid, low], axis=0)


def factor_kernel(x_ref, out_ref, perm_ref, y_ref, a_ref, row_ref, w_ref):
    rank, size = x_ref.shape
    steps = size // LANES
    f32 = jnp.float32
    for m in range(steps):
        col = lax.broadcasted_iota(jnp.int32, (size, LANES), 0)
        run = lax.broadcasted_iota(jnp.int32, (size, LANES), 1)
        perm_ref[:, m * LANES:(m + 1) * LANES] = jnp.where(col == run * steps + m, 1.0, 0.0).astype(jnp.bfloat16)
    x = x_ref[...]
    y = jnp.dot(x, perm_ref[...], preferred_element_type=f32)
    for m in range(steps):
        y_ref[m] = y[:, m * LANES:(m + 1) * LANES]
    mu = (damp_share / size) * jnp.sum(jnp.sum(y * y, axis=0, keepdims=True), axis=1, keepdims=True)
    for i in range(rank):
        acc = y_ref[0, pl.ds(i, 1), :] * y_ref[0]
        for m in range(1, steps):
            acc = acc + y_ref[m, pl.ds(i, 1), :] * y_ref[m]
        a_ref[i] = acc
    before = lax.broadcasted_iota(jnp.int32, (LANES, LANES), 0) < lax.broadcasted_iota(jnp.int32, (LANES, LANES), 1)
    prefix = jnp.dot(
        a_ref[...].reshape(rank * rank, LANES),
        before.astype(f32),
        precision=lax.Precision.HIGHEST,
        preferred_element_type=f32,
    ).reshape(rank, rank, LANES)
    sub = lax.broadcasted_iota(jnp.int32, (rank, LANES), 0)
    inv_mu = 1.0 / mu
    for i in range(rank):
        a_ref[i] = prefix[i] * inv_mu + jnp.where(sub == i, 1.0, 0.0)

    def sweep(p, carry):
        row_ref[0] = a_ref[p]
        inv_d = 1.0 / row_ref[0, pl.ds(p, 1), :]
        scaled = row_ref[0] * inv_d
        row_ref[1] = scaled
        at = sub == p
        for i in range(rank):
            a_ref[i] = jnp.where(at, row_ref[1, pl.ds(i, 1), :], a_ref[i] - row_ref[0, pl.ds(i, 1), :] * scaled)
        a_ref[p] = jnp.where(at, -inv_d, scaled)
        return carry

    lax.fori_loop(0, rank, sweep, 0)
    unit = rank ** -0.5
    for m in range(steps):
        v = y_ref[m]
        u = -a_ref[0] * y_ref[m, pl.ds(0, 1), :]
        for j in range(1, rank):
            u = u - a_ref[j] * y_ref[m, pl.ds(j, 1), :]
        d = mu + jnp.sum(v * u, axis=0, keepdims=True)
        inv_root = 1.0 / jnp.sqrt(d)
        g = u * inv_root
        lanes = pl.ds(m * LANES, LANES)
        w_ref[pl.ds(0, rank), lanes] = g * unit
        w_ref[pl.ds(rank, 8), lanes] = jnp.broadcast_to(mu * inv_root * unit, (8, LANES))
        if m < steps - 1:
            row_ref[0] = g
            for i in range(rank):
                a_ref[i] = a_ref[i] + row_ref[0, pl.ds(i, 1), :] * g
    natural = lax.dot_general(
        parts3(w_ref[...]), perm_ref[...], (((1,), (1,)), ((), ())), preferred_element_type=f32
    )
    tall = rank + 8
    diag = sum(natural[p * tall + rank:p * tall + rank + 1] for p in range(3))
    left = jnp.concatenate([natural[p * tall:p * tall + rank] for p in range(3)], axis=0).astype(jnp.bfloat16)
    right = jnp.concatenate([x, x, x], axis=0)
    for b in range(steps):
        lo = b * LANES
        block = lax.dot_general(
            left[:, lo:lo + LANES], right[:, lo:], (((0,), (0,)), ((), ())), preferred_element_type=f32
        )
        here = lax.broadcasted_iota(jnp.int32, (LANES, size - lo), 0)
        there = lax.broadcasted_iota(jnp.int32, (LANES, size - lo), 1)
        kept = jnp.where(there > here, block, 0.0)
        out_ref[pl.ds(lo, LANES), pl.ds(lo, size - lo)] = jnp.where(there == here, block + diag[:, lo:], kept)
        if b:
            out_ref[pl.ds(lo, LANES), pl.ds(0, lo)] = jnp.zeros((LANES, lo), f32)


def damped_factor(rows):
    rank, size = rows.shape
    if rank > RANK_MAX or rank % 16 or size % LANES:
        gram = lax.dot_general(rows, rows, (((0,), (0,)), ((), ())), preferred_element_type=jnp.float32)
        hess = gram / rank
        hess = hess + damp_share * jnp.mean(jnp.diagonal(hess)) * jnp.eye(size, dtype=jnp.float32)
        return jnp.linalg.cholesky(hess).T
    return pl.pallas_call(
        factor_kernel,
        out_shape=jax.ShapeDtypeStruct((size, size), jnp.float32),
        in_specs=[pl.BlockSpec(memory_space=pltpu.VMEM)],
        out_specs=pl.BlockSpec(memory_space=pltpu.VMEM),
        scratch_shapes=[
            pltpu.VMEM((size, size), jnp.bfloat16),
            pltpu.VMEM((size // LANES, rank, LANES), jnp.float32),
            pltpu.VMEM((rank, rank, LANES), jnp.float32),
            pltpu.VMEM((2, rank, LANES), jnp.float32),
            pltpu.VMEM((rank + 8, size), jnp.float32),
        ],
        compiler_params=pltpu.CompilerParams(vmem_limit_bytes=24 * 2**20),
        name="factor",
    )(rows)


def shifted(value, axis, by):
    devices = lax.axis_size(axis)
    pairs = [(i, i + by) for i in range(devices) if 0 <= i + by < devices]
    return lax.ppermute(value, axis, pairs)


def local(inputs, weights, keep_mask, gains):
    segment_count = lax.axis_size("segment")
    segment_idx = lax.axis_index("segment")
    tok_idx = lax.axis_index("tok")
    micro_count, row_count, width = inputs.shape
    col_width = weights.shape[2]
    nblk = keep_mask.shape[1]
    blk_size = width // nblk
    col_blocks = keep_mask.shape[2]
    block_mask = keep_mask[0].astype(jnp.bfloat16)
    pruned = (
        weights[0].reshape(nblk, blk_size, col_blocks, blk_size) * block_mask[:, None, :, None]
    ).reshape(width, col_width)
    gain_row = gains[0][None, :]
    col_start = tok_idx * col_width
    current = inputs.reshape(micro_count * row_count, width)
    stored = jnp.zeros_like(current)
    group = None
    for tick_num in range(segment_count):
        mine = segment_idx == tick_num
        whole = lax.all_gather(current, "tok", axis=0, tiled=True)
        group_now = whole[:, :GRP]
        group = group_now if group is None else jnp.where(mine, group_now, group)
        row_vals = whole.astype(jnp.float32)
        mean_sq = jnp.mean(row_vals * row_vals, axis=-1, keepdims=True)
        normed = (row_vals * lax.rsqrt(mean_sq + norm_eps) * gain_row).astype(jnp.bfloat16)
        product = jnp.dot(normed, pruned, preferred_element_type=jnp.float32)
        resid_cols = lax.dynamic_slice_in_dim(row_vals, col_start, col_width, 1)
        new_cols = (resid_cols + product).astype(jnp.bfloat16)
        output = lax.all_to_all(new_cols, "tok", split_axis=0, concat_axis=1, tiled=True)
        stored = jnp.where(mine, output, stored)
        if tick_num < segment_count - 1:
            current = shifted(output, "segment", 1)
    return (stored.reshape((1,) + inputs.shape), damped_factor(group)[None])


def solution(mesh):
    return jax.shard_map(
        local,
        mesh=mesh,
        in_specs=(
            P(None, "tok", None),
            P("segment", None, "tok"),
            P("segment", None, "tok"),
            P("segment", None),
        ),
        out_specs=(P("segment", None, "tok", None), P("segment", None, None)),
        check_vma=False,
    )
```

time: 582 us -> 174 us (0.30); the launches traced: 571 us -> 171 us
  other arithmetic: 196 us -> 8.08 us
  waiting for transfers between devices: 124 us -> 11.7 us
  matrix products: 84.1 us -> 35.3 us
  local copies, waits for them, and re-layouts: 44 us -> 8.65 us
  between operations: 20.3 us -> 0.81 us
  starting transfers between devices: 23.6 us -> 7.26 us
  blocking collectives: 79 us -> 90.4 us
  Pallas kernels: 0 us -> 8.81 us
    another operation x30 -> x0, other arithmetic: 168 us -> none  [local(): factor = jnp.linalg.cholesky(hess).T]
    psum x1 -> x0, waiting for transfers between devices: 99.7 us -> none  [local(): total = lax.psum(gram, 'tok')]
    another operation x14 -> x0, matrix products: 27.1 us -> none  [local(): factor = jnp.linalg.cholesky(hess).T]
    all_to_all x0 -> x3, blocking collectives: none -> 24.9 us  [local(): lax.all_to_all(new_cols, 'tok', split_axis=0, concat_axis=1, tiled=True)]
    gather x1 -> x0, local copies, waits for them, and re-layouts: 17 us -> none  [local(): damp_val = damp_share * jnp.mean(jnp.diagonal(hess))]
    all_to_all x5 -> x1, waiting for transfers between devices: 17 us -> 0.01 us  [local(): lax.all_to_all(new_cols, 'tok', split_axis=0, concat_axis=1, tiled=True)]
    dot_general x5 -> x0, matrix products: 16.5 us -> none  [local(): lax.dot_general(group_cols, group_cols, (((0,), (0,)), ((), ())), preferr...]
    all_to_all x5 -> x1, starting transfers between devices: 18.5 us -> 3.42 us  [local(): lax.all_to_all(new_cols, 'tok', split_axis=0, concat_axis=1, tiled=True)]
  transfers between devices with their start and end apart: 10 -> 4, of which waited for: 9 -> 3; matrix products, arithmetic and copies ran while one was open for 3% -> 0% of each run, Pallas kernels for 0% -> 5%
where the time goes in v1:
time: 174 us; the launch traced here: 171 us
  blocking collectives  90.4 us (52%)
  matrix products  35.3 us (20%)
  waiting for transfers between devices  11.7 us (7%)
  Pallas kernels  8.81 us (5%)
  local copies, waits for them, and re-layouts  8.65 us (5%)
  other arithmetic  8.08 us (5%)
  starting transfers between devices  7.26 us (4%)
    all_gather x4, blocking collectives, local(): whole = lax.all_gather(current, 'tok', axis=0, tiled=True)  65.5 us
    dot_general x4, matrix products, local(): product = jnp.dot(normed, pruned, preferred_element_type=jnp.float32)  35.3 us
    all_to_all x3, blocking collectives, local(): lax.all_to_all(new_cols, 'tok', split_axis=0, concat_axis=1, tiled=True)  24.9 us
    ppermute x3, waiting for transfers between devices, shifted(): return lax.ppermute(value, axis, pairs)  11.7 us
    pallas_call x1, Pallas kernels, damped_factor(): pl.pallas_call(factor_kernel, out_shape=jax.ShapeDtypeStruct((size, size)...  8.81 us
    mul x1, other arithmetic, local(): weights[0].reshape(nblk, blk_size, col_blocks, blk_size)  6.05 us
    unnamed x9, local copies, waits for them, and re-layouts  4.28 us
    ppermute x3, starting transfers between devices, shifted(): return lax.ppermute(value, axis, pairs)  3.84 us
  transfers between devices with their start and end apart: 4, of which 3 were waited for; matrix products, arithmetic and copies ran while one was open for 0% of the time, Pallas kernels for 5%

profile of v1, /device:TPU:7, one launch (start us, length us, event | category | flops | bytes accessed | tf_op | source)
XLA Modules:
  0.0 171.0 jit_solution(10634653641488097374)
XLA Ops:
  0.6 0.9 reshape.111
  1.5 15.5 %all-gather = bf16[8,4,8192]{2,1,0:T(4,128)(2,1)S(1)} all-gather(bf16[1,4,8192]{2,1,0:T(4,128)(2,1)S(1)} %reshape.111), channel_id=1, replica_groups=mesh['segment'=4,'tok'=8] {'tok'}, dimensions={0}, use_global_device_ids=true | all-gather | bytes 589824 | tf_op jit(solution)/shard_map/all_gather | solution.py:155
  17.0 0.1 reshape.112
  17.2 0.2 multiply_reduce_fusion.3
  17.4 0.1 convert_element_type.46
  17.5 0.7 convert_bitcast_fusion
  18.2 0.1 copy.8
  18.3 0.0 copy-start
  18.3 2.8 %mul.93 = bf16[64,128,8,128]{3,2,1,0:T(8,128)(2,1)S(1)} broadcast(bf16[64,8]{1,0:T(8,128)(2,1)S(1)} %copy.8), dimensions={0,2} | broadcast | bytes 16778240 | tf_op jit(solution)/shard_map/mul | solution.py:146
  21.1 2.9 %copy-done = bf16[1,8192,1024]{2,1,0:T(8,128)(2,1)S(1)} copy-done((bf16[1,8192,1024]{2,1,0:T(8,128)(2,1)S(1)}, bf16[1,8192,1024]{2,1,0:T(8,128)(2,1)}, u32[]{:S(2)}) %copy-start) | copy-done | bytes 16777240
  24.1 0.0 copy-start.1
  24.1 6.0 %bitcast_multiply_fusion = bf16[8192,1024]{1,0:T(8,128)(2,1)} fusion(bf16[1024,8,8,128]{3,2,1,0:T(8,128)(2,1)S(1)} %bitcast.37, bf16[1,8192,1024]{2,1,0:T(8,128)(2,1)S(1)} %copy-done), kind=kLoop, calls=%fused_computation | loop fusion | flops 8388608 | bytes 50331648 | tf_op jit(solution)/shard_map/mul | solution.py:146
  30.1 0.0 copy-done.1
  30.1 8.8 %fusion = bf16[32,1024]{1,0:T(8,128)(2,1)S(1)} fusion(bf16[8192,1024]{1,0:T(8,128)(2,1)} %bitcast_multiply_fusion, f32[8192]{0:T(1024)S(1)} %bitcast.39, f32[32]{0:T(128)S(1)} %add_rsqrt_fusion.3, bf16[32,8192]{1,0:T(8,128)(2,1)S(1)} %reshape.112, f32[32,8192]{1,0:T(8,128)S(1)} %convert_element_type.46, s32[]{:T(128)S(6)} %select_n.87), kind=kOutput, calls=%fused_computation.2 | convolution fusion | flops 537985024 | bytes 17531012 | tf_op jit(solution)/shard_map/dot_general | solution.py:161
  39.0 9.7 %all_to_all.73 = bf16[8,4,1024]{2,1,0:T(4,128)(2,1)S(1)} all-to-all(bf16[8,4,1024]{2,1,0:T(4,128)(2,1)S(1)} %all_to_all.54), channel_id=1, replica_groups=mesh['segment'=4,'tok'=8] {'tok'}, dimensions={0} | all-to-all | bytes 131072 | tf_op jit(solution)/shard_map/all_to_all | solution.py:164
  48.7 1.3 collective-permute-start
  50.0 3.7 %collective-permute-done = bf16[4,8192]{1,0:T(4,128)(2,1)S(1)} collective-permute-done((bf16[4,8192]{1,0:T(4,128)(2,1)S(1)}, bf16[4,8192]{1,0:T(4,128)(2,1)S(1)}, u32[]{:S(2)}, u32[]{:S(2)}) %collective-permute-start) | collective-permute-done | bytes 65568 | tf_op jit(solution)/shard_map/ppermute | solution.py:132
  53.7 16.7 %all-gather.1 = bf16[8,4,8192]{2,1,0:T(4,128)(2,1)S(1)} all-gather(bf16[1,4,8192]{2,1,0:T(4,128)(2,1)S(1)} %bitcast.47), channel_id=1, replica_groups=mesh['segment'=4,'tok'=8] {'tok'}, dimensions={0}, use_global_device_ids=true | all-gather | bytes 589824 | tf_op jit(solution)/shard_map/all_gather | solution.py:155
  70.4 0.1 reshape.114
  70.5 0.1 convert_element_type.51
  70.6 0.2 multiply_reduce_fusion.2
  70.8 8.8 %add_convert_fusion.2 = bf16[32,1024]{1,0:T(8,128)(2,1)S(1)} fusion(f32[32,8192]{1,0:T(8,128)S(1)} %convert_element_type.51, s32[]{:T(128)S(6)} %select_n.87, bf16[8192,1024]{1,0:T(8,128)(2,1)} %bitcast_multiply_fusion, f32[32]{0:T(128)S(1)} %add_rsqrt_fusion.2, bf16[32,8192]{1,0:T(8,128)(2,1)S(1)} %reshape.114, f32[8192]{0:T(1024)S(1)} %bitcast.40), kind=kOutput, calls=%fused_computation.28 | convolution fusion | flops 537985024 | bytes 17531012 | tf_op jit(solution)/shard_map/dot_general | solution.py:161
  79.7 7.6 %all_to_all.74 = bf16[8,4,1024]{2,1,0:T(4,128)(2,1)S(1)} all-to-all(bf16[8,4,1024]{2,1,0:T(4,128)(2,1)S(1)} %all_to_all.58), channel_id=1, replica_groups=mesh['segment'=4,'tok'=8] {'tok'}, dimensions={0} | all-to-all | bytes 131072 | tf_op jit(solution)/shard_map/all_to_all | solution.py:164
  87.3 1.3 collective-permute-start.1
  88.6 3.7 %collective-permute-done.1 = bf16[4,8192]{1,0:T(4,128)(2,1)S(1)} collective-permute-done((bf16[4,8192]{1,0:T(4,128)(2,1)S(1)}, bf16[4,8192]{1,0:T(4,128)(2,1)S(1)}, u32[]{:S(2)}, u32[]{:S(2)}) %collective-permute-start.1) | collective-permute-done | bytes 65568 | tf_op jit(solution)/shard_map/ppermute | solution.py:132
  92.3 16.7 %all-gather.2 = bf16[8,4,8192]{2,1,0:T(4,128)(2,1)S(1)} all-gather(bf16[1,4,8192]{2,1,0:T(4,128)(2,1)S(1)} %bitcast.48), channel_id=1, replica_groups=mesh['segment'=4,'tok'=8] {'tok'}, dimensions={0}, use_global_device_ids=true | all-gather | bytes 589824 | tf_op jit(solution)/shard_map/all_gather | solution.py:155
  109.0 0.1 reshape.116
  109.1 0.1 convert_element_type.54
  109.2 0.2 multiply_reduce_fusion.1
  109.4 8.8 %add_convert_fusion.1 = bf16[32,1024]{1,0:T(8,128)(2,1)S(1)} fusion(f32[32,8192]{1,0:T(8,128)S(1)} %convert_element_type.54, s32[]{:T(128)S(6)} %select_n.87, bf16[8192,1024]{1,0:T(8,128)(2,1)} %bitcast_multiply_fusion, f32[32]{0:T(128)S(1)} %add_rsqrt_fusion.1, bf16[32,8192]{1,0:T(8,128)(2,1)S(1)} %reshape.116, f32[8192]{0:T(1024)S(1)} %bitcast.41), kind=kOutput, calls=%fused_computation.27 | convolution fusion | flops 537985024 | bytes 17531012 | tf_op jit(solution)/shard_map/dot_general | solution.py:161
  118.3 7.6 %all_to_all.75 = bf16[8,4,1024]{2,1,0:T(4,128)(2,1)S(1)} all-to-all(bf16[8,4,1024]{2,1,0:T(4,128)(2,1)S(1)} %all_to_all.62), channel_id=1, replica_groups=mesh['segment'=4,'tok'=8] {'tok'}, dimensions={0} | all-to-all | bytes 131072 | tf_op jit(solution)/shard_map/all_to_all | solution.py:164
  125.9 1.3 collective-permute-start.2
  127.2 4.3 %collective-permute-done.2 = bf16[4,8192]{1,0:T(4,128)(2,1)S(1)} collective-permute-done((bf16[4,8192]{1,0:T(4,128)(2,1)S(1)}, bf16[4,8192]{1,0:T(4,128)(2,1)S(1)}, u32[]{:S(2)}, u32[]{:S(2)}) %collective-permute-start.2) | collective-permute-done | bytes 65568 | tf_op jit(solution)/shard_map/ppermute | solution.py:132
  131.5 16.6 %all-gather.3 = bf16[8,4,8192]{2,1,0:T(4,128)(2,1)S(1)} all-gather(bf16[1,4,8192]{2,1,0:T(4,128)(2,1)S(1)} %bitcast.46), channel_id=1, replica_groups=mesh['segment'=4,'tok'=8] {'tok'}, dimensions={0}, use_global_device_ids=true | all-gather | bytes 589824 | tf_op jit(solution)/shard_map/all_gather | solution.py:155
  148.1 0.1 reshape.118
  148.2 0.1 convert_element_type.57
  148.3 0.2 multiply_reduce_fusion
  148.5 8.8 %add_convert_fusion = bf16[32,1024]{1,0:T(8,128)(2,1)S(1)} fusion(f32[32,8192]{1,0:T(8,128)S(1)} %convert_element_type.57, s32[]{:T(128)S(6)} %select_n.87, bf16[8192,1024]{1,0:T(8,128)(2,1)} %bitcast_multiply_fusion, f32[32]{0:T(128)S(1)} %add_rsqrt_fusion, bf16[32,8192]{1,0:T(8,128)(2,1)S(1)} %reshape.118, f32[8192]{0:T(1024)S(1)} %bitcast.42), kind=kOutput, calls=%fused_computation.26 | convolution fusion | flops 537985024 | bytes 17531012 | tf_op jit(solution)/shard_map/dot_general | solution.py:161
  157.3 0.7 all_to_all.66
  158.0 3.4 %all-to-all-start.3 = ((bf16[8,4,1024]{2,1,0:T(4,128)(2,1)}), bf16[8,4,1024]{2,1,0:T(4,128)(2,1)S(1)}, u32[]{:S(2)}, u32[]{:S(2)}) async-start(bf16[8,4,1024]{2,1,0:T(4,128)(2,1)} %all_to_all.66), calls=%async_computation.3 | async-start | bytes 131072 | tf_op jit(solution)/shard_map/all_to_all | solution.py:164
  161.4 8.8 %factor.1 = f32[1024,1024]{1,0:T(8,128)} custom-call(bf16[32,1024]{1,0:T(8,128)(2,1)S(1)} %fusion.17.x_ref), custom_call_target="tpu_custom_call" | custom-call | tf_op jit(solution)/shard_map/factor/pallas_call | solution.py:112
  170.3 0.0 all-to-all-done.3
  170.3 0.1 bitcast_select_fusion
  170.4 0.7 select_n.95
  (9 shorter events, 0.2 us)
Async XLA Ops:
  18.3 5.8 %copy-start = (bf16[1,8192,1024]{2,1,0:T(8,128)(2,1)S(1)}, bf16[1,8192,1024]{2,1,0:T(8,128)(2,1)}, u32[]{:S(2)}) copy-start(bf16[1,8192,1024]{2,1,0:T(8,128)(2,1)} %param.5) | copy-start | bytes 50331652
  24.1 6.1 %copy-start.1 = (f32[1,8192]{1,0:T(1,128)S(1)}, f32[1,8192]{1,0:T(1,128)}, u32[]{:S(2)}) copy-start(f32[1,8192]{1,0:T(1,128)} %param.7) | copy-start | bytes 98308
  48.7 5.0 %collective-permute-start = (bf16[4,8192]{1,0:T(4,128)(2,1)S(1)}, bf16[4,8192]{1,0:T(4,128)(2,1)S(1)}, u32[]{:S(2)}, u32[]{:S(2)}) collective-permute-start(bf16[4,8192]{1,0:T(4,128)(2,1)S(1)} %bitcast.43), channel_id=1, source_target_pairs={{0,8},{8,16},{16,24},{1,9},{9,17},{17,25},{2,10},{10,18},{18,26},{... | collective-permute-start | bytes 196616 | tf_op jit(solution)/shard_map/ppermute | solution.py:132
  87.3 5.0 %collective-permute-start.1 = (bf16[4,8192]{1,0:T(4,128)(2,1)S(1)}, bf16[4,8192]{1,0:T(4,128)(2,1)S(1)}, u32[]{:S(2)}, u32[]{:S(2)}) collective-permute-start(bf16[4,8192]{1,0:T(4,128)(2,1)S(1)} %bitcast.44), channel_id=1, source_target_pairs={{0,8},{8,16},{16,24},{1,9},{9,17},{17,25},{2,10},{10,18},{18,26},{... | collective-permute-start | bytes 196616 | tf_op jit(solution)/shard_map/ppermute | solution.py:132
  125.9 5.6 %collective-permute-start.2 = (bf16[4,8192]{1,0:T(4,128)(2,1)S(1)}, bf16[4,8192]{1,0:T(4,128)(2,1)S(1)}, u32[]{:S(2)}, u32[]{:S(2)}) collective-permute-start(bf16[4,8192]{1,0:T(4,128)(2,1)S(1)} %bitcast.45), channel_id=1, source_target_pairs={{0,8},{8,16},{16,24},{1,9},{9,17},{17,25},{2,10},{10,18},{18,26},{... | collective-permute-start | bytes 196616 | tf_op jit(solution)/shard_map/ppermute | solution.py:132
  158.0 12.3 %all-to-all-start.3 = ((bf16[8,4,1024]{2,1,0:T(4,128)(2,1)}), bf16[8,4,1024]{2,1,0:T(4,128)(2,1)S(1)}, u32[]{:S(2)}, u32[]{:S(2)}) async-start(bf16[8,4,1024]{2,1,0:T(4,128)(2,1)} %all_to_all.66), calls=%async_computation.3 | async-start | bytes 131072 | tf_op jit(solution)/shard_map/all_to_all | solution.py:164

commit v2 on v1

--- a/solution.py
+++ b/solution.py
@@ -132,7 +132,7 @@
     return lax.ppermute(value, axis, pairs)
 
 
-def local(inputs, weights, keep_mask, gains):
+def local_xla(inputs, weights, keep_mask, gains):
     segment_count = lax.axis_size("segment")
     segment_idx = lax.axis_index("segment")
     tok_idx = lax.axis_index("tok")
@@ -167,6 +167,232 @@
             current = shifted(output, "segment", 1)
     return (stored.reshape((1,) + inputs.shape), damped_factor(group)[None])
 
+def forward_kernel(
+    x_in, w_hbm, keep, gain, acts, group,
+    w_buf, x_buf, rows_buf, rows_f32, mask_row, acc, sq_sum, y_send, y_rows, out_rows,
+    w_sem, next_send, x_recv, relay_send, a_send, a_recv,
+):
+    f32 = jnp.float32
+    segments, toks = lax.axis_size("segment"), lax.axis_size("tok")
+    seg, tok = lax.axis_index("segment"), lax.axis_index("tok")
+    pairs = toks // 2
+    pair, core = tok // 2, tok % 2
+    sister = tok + 1 - 2 * core
+    micro, piece, width = x_in.shape
+    _, rows, cols = x_buf.shape
+    nblk, col_blocks = keep.shape[1:]
+    blk = width // nblk
+    per_chunk = nblk // toks
+
+    def place(step, which):
+        return lax.rem(pair + step, pairs) * 2 + which
+
+    def remote(src, dst, send, recv, to_seg, to_tok):
+        return pltpu.make_async_remote_copy(
+            src_ref=src, dst_ref=dst, send_sem=send, recv_sem=recv,
+            device_id=(to_seg, to_tok), device_id_type=pl.DeviceIdType.MESH,
+        )
+
+    def w_copy(k):
+        return pltpu.make_async_copy(w_hbm.at[0, pl.ds(k * cols, cols), :], w_buf.at[k], w_sem.at[k])
+
+    for k in range(toks):
+        w_copy(k).start()
+
+    barrier = pltpu.get_barrier_semaphore()
+
+    def greet(to_seg, to_tok):
+        pl.semaphore_signal(barrier, inc=1, device_id=(to_seg, to_tok), device_id_type=pl.DeviceIdType.MESH)
+
+    for k in range(1, toks):
+        greet(seg, lax.rem(tok + k, toks))
+
+    @pl.when(seg > 0)
+    def _():
+        for k in range(pairs):
+            greet(seg - 1, place(k, core))
+
+    @pl.when(seg < segments - 1)
+    def _():
+        for k in range(pairs):
+            greet(seg + 1, place(k, core))
+
+    before = jnp.where(seg > 0, pairs, 0)
+    after = jnp.where(seg < segments - 1, pairs, 0)
+    pl.semaphore_wait(barrier, toks - 1 + before + after)
+
+    def first_copy(k):
+        to = sister if k == 0 else place(k, core)
+        return remote(x_in, rows_buf.at[tok], next_send.at[k], x_recv.at[tok], seg, to)
+
+    @pl.when(seg == 0)
+    def _():
+        for k in range(pairs):
+            first_copy(k).start()
+
+    spread = lax.broadcasted_iota(jnp.int32, (col_blocks, cols), 1) // blk
+    spread = jnp.where(spread == lax.broadcasted_iota(jnp.int32, (col_blocks, cols), 0), 1.0, 0.0)
+    mask_row[...] = jnp.dot(
+        keep[0].astype(f32).astype(jnp.bfloat16), spread.astype(jnp.bfloat16), preferred_element_type=f32
+    )
+
+    def prune(k, carry):
+        w_copy(k).wait()
+        for b in range(per_chunk):
+            kept = jnp.broadcast_to(mask_row[pl.ds(k * per_chunk + b, 1), :], (16, cols)).astype(jnp.bfloat16)
+            block = w_buf[k, pl.ds(b * blk, blk), :].reshape(blk // 16, 16, cols)
+            w_buf[k, pl.ds(b * blk, blk), :] = (block * kept[None]).reshape(blk, cols)
+        return carry
+
+    lax.fori_loop(0, toks, prune, 0)
+    acc[...] = jnp.zeros_like(acc)
+    sq_sum[...] = jnp.zeros_like(sq_sum)
+
+    def relay(buf, k, src):
+        return remote(buf.at[src], buf.at[src], relay_send.at[k], x_recv.at[src], seg, sister)
+
+    def step(src):
+        x = x_buf[src].astype(f32)
+        sq = x * x
+        part = sq[:, :LANES]
+        for lo in range(LANES, cols, LANES):
+            part = part + sq[:, lo:lo + LANES]
+        sq_sum[...] += part
+        gained = (x * gain[0:1, pl.ds(pl.multiple_of(src * cols, cols), cols)]).astype(jnp.bfloat16)
+        acc[...] += jnp.dot(gained, w_buf[src], preferred_element_type=f32)
+
+    @pl.when(seg == 0)
+    def _():
+        rows_buf[tok] = x_in[...]
+        for k in range(1, pairs):
+            src = place(pairs - k, core)
+            relay(rows_buf, k, src).wait_recv()
+            relay(rows_buf, k, src).start()
+        for k in range(pairs):
+            relay(rows_buf, k, place(pairs - k, 1 - core)).wait_recv()
+        for t in range(toks):
+            for m in range(micro):
+                rows_f32[pl.ds((t * micro + m) * piece, piece), :] = rows_buf[t, m].astype(f32)
+        for t in range(toks):
+            x_buf[t] = rows_f32[:, t * cols:(t + 1) * cols].astype(jnp.bfloat16)
+
+        def one(src, carry):
+            step(src)
+            return carry
+
+        lax.fori_loop(0, toks, one, 0)
+        for k in range(pairs):
+            first_copy(k).wait_send()
+        for k in range(1, pairs):
+            relay(rows_buf, k, place(pairs - k, core)).wait_send()
+
+    @pl.when(seg > 0)
+    def _():
+        def direct(k, carry):
+            src = place(k, core)
+            relay(x_buf, k, src).wait_recv()
+            relay(x_buf, k, src).start()
+            step(src)
+            return carry
+
+        lax.fori_loop(0, pairs, direct, 0)
+
+        def relayed(k, carry):
+            src = place(k, 1 - core)
+            relay(x_buf, k, src).wait_recv()
+            step(src)
+            return carry
+
+        lax.fori_loop(0, pairs, relayed, 0)
+        for k in range(pairs):
+            relay(x_buf, k, place(k, core)).wait_send()
+
+    mean_sq = jnp.sum(sq_sum[...], axis=1, keepdims=True) * (1.0 / width)
+    y = x_buf[tok].astype(f32) + acc[...] * lax.rsqrt(mean_sq + norm_eps)
+    y_send[...] = y.astype(jnp.bfloat16)
+
+    def next_copy(k):
+        return remote(y_send, x_buf.at[tok], next_send.at[k], x_recv.at[tok], seg + 1, place(k, core))
+
+    @pl.when(seg < segments - 1)
+    def _():
+        for k in range(pairs):
+            next_copy(k).start()
+
+    acc[...] = y
+    for t in range(toks):
+        for m in range(micro):
+            y_rows[t, m] = acc[pl.ds((t * micro + m) * piece, piece), :].astype(jnp.bfloat16)
+
+    def a_copy(k):
+        to = lax.rem(tok + k, toks)
+        return remote(y_rows.at[to], out_rows.at[tok], a_send.at[k], a_recv.at[tok], seg, to)
+
+    for k in range(1, toks):
+        a_copy(k).start()
+    for t in range(group.shape[1] // cols):
+        group[:, t * cols:(t + 1) * cols] = x_buf[t]
+    out_rows[tok] = y_rows[tok]
+    for k in range(1, toks):
+        src = lax.rem(tok + toks - k, toks)
+        remote(y_rows.at[src], out_rows.at[src], a_send.at[k], a_recv.at[src], seg, src).wait_recv()
+    for t in range(toks):
+        acts[0, :, :, t * cols:(t + 1) * cols] = out_rows[t]
+    for k in range(1, toks):
+        a_copy(k).wait_send()
+
+    @pl.when(seg < segments - 1)
+    def _():
+        for k in range(pairs):
+            next_copy(k).wait_send()
+
+
+def local_kernel(inputs, weights, keep_mask, gains):
+    toks = lax.axis_size("tok")
+    micro, piece, width = inputs.shape
+    cols = weights.shape[2]
+    nblk = keep_mask.shape[1]
+    rows = micro * piece * toks
+    vmem = pl.BlockSpec(memory_space=pltpu.VMEM)
+    bf16, f32 = jnp.bfloat16, jnp.float32
+    dma = pltpu.SemaphoreType.DMA
+    acts, group = pl.pallas_call(
+        forward_kernel,
+        out_shape=(
+            jax.ShapeDtypeStruct((1,) + inputs.shape, bf16),
+            jax.ShapeDtypeStruct((rows, min(GRP, width)), bf16),
+        ),
+        in_specs=[vmem, pl.BlockSpec(memory_space=pltpu.HBM), vmem, vmem],
+        out_specs=(vmem, vmem),
+        scratch_shapes=[
+            pltpu.VMEM((toks, width // toks, cols), bf16),
+            pltpu.VMEM((toks, rows, cols), bf16),
+            pltpu.VMEM((toks, micro, piece, width), bf16),
+            pltpu.VMEM((rows, width), f32),
+            pltpu.VMEM((nblk, cols), f32),
+            pltpu.VMEM((rows, cols), f32),
+            pltpu.VMEM((rows, LANES), f32),
+            pltpu.VMEM((rows, cols), bf16),
+            pltpu.VMEM((toks, micro, piece, cols), bf16),
+            pltpu.VMEM((toks, micro, piece, cols), bf16),
+            dma((toks,)), dma((toks,)), dma((toks,)), dma((toks,)), dma((toks,)), dma((toks,)),
+        ],
+        compiler_params=pltpu.CompilerParams(
+            collective_id=0, has_side_effects=True, vmem_limit_bytes=48 * 2**20
+        ),
+        name="forward",
+    )(inputs, weights, keep_mask, gains)
+    return (acts, damped_factor(group)[None])
+
+
+def local(inputs, weights, keep_mask, gains):
+    toks = lax.axis_size("tok")
+    rows = inputs.shape[0] * inputs.shape[1] * toks
+    width, cols = weights.shape[1:]
+    if rows > RANK_MAX or rows % 16 or toks % 2 or cols % LANES or GRP % cols:
+        return local_xla(inputs, weights, keep_mask, gains)
+    return local_kernel(inputs, weights, keep_mask, gains)
+
 
 def solution(mesh):
     return jax.shard_map(

time: 174 us -> 67.2 us (0.39); the launches traced: 171 us -> 66.9 us
  blocking collectives: 90.4 us -> 0 us
  Pallas kernels: 8.81 us -> 63.3 us
  matrix products: 35.3 us -> 0 us
  waiting for transfers between devices: 11.7 us -> 0 us
  other arithmetic: 8.08 us -> 0 us
  starting transfers between devices: 7.26 us -> 0 us
  local copies, waits for them, and re-layouts: 8.65 us -> 3 us
    all_gather x4 -> x0, blocking collectives: 65.5 us -> none  [local(): whole = lax.all_gather(current, 'tok', axis=0, tiled=True)]
    pallas_call x0 -> x1, Pallas kernels: none -> 54.5 us  [local_kernel(): pl.pallas_call(forward_kernel, out_shape=(jax.ShapeDtypeStruct((1,) + inp...]
    dot_general x4 -> x0, matrix products: 35.3 us -> none  [local(): product = jnp.dot(normed, pruned, preferred_element_type=jnp.float32)]
    all_to_all x3 -> x0, blocking collectives: 24.9 us -> none  [local(): lax.all_to_all(new_cols, 'tok', split_axis=0, concat_axis=1, tiled=True)]
    ppermute x3 -> x0, waiting for transfers between devices: 11.7 us -> none  [shifted(): return lax.ppermute(value, axis, pairs)]
    mul x1 -> x0, other arithmetic: 6.05 us -> none  [local(): weights[0].reshape(nblk, blk_size, col_blocks, blk_size)]
    ppermute x3 -> x0, starting transfers between devices: 3.84 us -> none  [shifted(): return lax.ppermute(value, axis, pairs)]
    all_to_all x1 -> x0, starting transfers between devices: 3.42 us -> none  [local(): lax.all_to_all(new_cols, 'tok', split_axis=0, concat_axis=1, tiled=True)]
  transfers between devices with their start and end apart: 4 -> 0, of which waited for: 3 -> 0; matrix products, arithmetic and copies ran while one was open for 0% -> 0% of each run, Pallas kernels for 5% -> 0%
where the time goes in v2:
time: 67.2 us; the launch traced here: 66.9 us
  Pallas kernels  63.3 us (94%)
  local copies, waits for them, and re-layouts  3 us (4%)
    pallas_call x1, Pallas kernels, local_kernel(): pl.pallas_call(forward_kernel, out_shape=(jax.ShapeDtypeStruct((1,) + inp...  54.5 us
    pallas_call x1, Pallas kernels, damped_factor(): pl.pallas_call(factor_kernel, out_shape=jax.ShapeDtypeStruct((size, size)...  8.81 us
    unnamed x6, local copies, waits for them, and re-layouts  3 us

profile of v2, /device:TPU:7, one launch (start us, length us, event | category | flops | bytes accessed | tf_op | source)
XLA Modules:
  0.0 66.9 jit_solution(7532329621543395075)
XLA Ops:
  0.6 0.8 %copy.6.keep = s32[1,64,8]{2,1,0:T(8,128)S(1)} copy(s32[1,64,8]{1,2,0:T(8,128)} %param.6) | data formatting | bytes 4096 | tf_op args[2]
  1.4 0.0 copy-start
  1.4 0.8 %copy-done = bf16[2,2,8192]{2,1,0:T(2,128)(2,1)S(1)} copy-done((bf16[2,2,8192]{2,1,0:T(2,128)(2,1)S(1)}, bf16[2,2,8192]{2,1,0:T(2,128)(2,1)}, u32[]{:S(2)}) %copy-start) | copy-done | bytes 65560
  2.2 0.0 copy-start.1
  2.2 0.8 %copy-done.1 = f32[1,8192]{1,0:T(1,128)S(1)} copy-done((f32[1,8192]{1,0:T(1,128)S(1)}, f32[1,8192]{1,0:T(1,128)}, u32[]{:S(2)}) %copy-start.1) | copy-done | bytes 32792
  3.0 54.5 %forward.1 = (bf16[1,2,2,8192]{3,2,1,0:T(2,128)(2,1)S(1)}, bf16[32,1024]{1,0:T(8,128)(2,1)S(1)}) custom-call(bf16[2,2,8192]{2,1,0:T(2,128)(2,1)S(1)} %copy-done, bf16[1,8192,1024]{2,1,0:T(8,128)(2,1)} %w_hbm.1, s32[1,64,8]{2,1,0:T(8,128)S(1)} %copy.6.keep, f32[1,8192]{1,0:T(1,128)S(1)} %copy-done.1), custom_call_target="tpu_custom_call" | custom-call | tf_op jit(solution)/shard_map/forward/pallas_call | solution.py:359
  57.5 8.8 %factor.1 = f32[1024,1024]{1,0:T(8,128)} custom-call(bf16[32,1024]{1,0:T(8,128)(2,1)S(1)} %get-tuple-element.5.x_ref), custom_call_target="tpu_custom_call" | custom-call | tf_op jit(solution)/shard_map/factor/pallas_call | solution.py:112
  66.3 0.6 copy.8
Async XLA Ops:
  1.4 0.8 %copy-start = (bf16[2,2,8192]{2,1,0:T(2,128)(2,1)S(1)}, bf16[2,2,8192]{2,1,0:T(2,128)(2,1)}, u32[]{:S(2)}) copy-start(bf16[2,2,8192]{2,1,0:T(2,128)(2,1)} %x_in.1) | copy-start | bytes 196612
  2.2 0.8 %copy-start.1 = (f32[1,8192]{1,0:T(1,128)S(1)}, f32[1,8192]{1,0:T(1,128)}, u32[]{:S(2)}) copy-start(f32[1,8192]{1,0:T(1,128)} %gain.1) | copy-start | bytes 98308

commit v3 on v2

--- a/solution.py
+++ b/solution.py
@@ -168,9 +168,9 @@
     return (stored.reshape((1,) + inputs.shape), damped_factor(group)[None])
 
 def forward_kernel(
-    x_in, w_hbm, keep, gain, acts, group,
+    x_in, w_hbm, keep, gain_hbm, acts, group, gain,
     w_buf, x_buf, rows_buf, rows_f32, mask_row, acc, sq_sum, y_send, y_rows, out_rows,
-    w_sem, next_send, x_recv, relay_send, a_send, a_recv,
+    in_sem, w_sem, next_send, x_recv, relay_send, a_send, a_recv,
 ):
     f32 = jnp.float32
     segments, toks = lax.axis_size("segment"), lax.axis_size("tok")
@@ -185,7 +185,7 @@
     per_chunk = nblk // toks
 
     def place(step, which):
-        return lax.rem(pair + step, pairs) * 2 + which
+        return jnp.where(2 * pair >= pairs, step, pairs - 1 - step) * 2 + which
 
     def remote(src, dst, send, recv, to_seg, to_tok):
         return pltpu.make_async_remote_copy(
@@ -196,6 +196,14 @@
     def w_copy(k):
         return pltpu.make_async_copy(w_hbm.at[0, pl.ds(k * cols, cols), :], w_buf.at[k], w_sem.at[k])
 
+    own_rows = pltpu.make_async_copy(x_in, rows_buf.at[tok], in_sem.at[0])
+    gain_copy = pltpu.make_async_copy(gain_hbm, gain, in_sem.at[1])
+    gain_copy.start()
+
+    @pl.when(seg == 0)
+    def _():
+        own_rows.start()
+
     for k in range(toks):
         w_copy(k).start()
 
@@ -221,14 +229,25 @@
     after = jnp.where(seg < segments - 1, pairs, 0)
     pl.semaphore_wait(barrier, toks - 1 + before + after)
 
-    def first_copy(k):
-        to = sister if k == 0 else place(k, core)
-        return remote(x_in, rows_buf.at[tok], next_send.at[k], x_recv.at[tok], seg, to)
+    def first_copy(to):
+        return remote(x_in, rows_buf.at[tok], next_send.at[to // 2], x_recv.at[tok], seg, to)
+
+    def first_start(to):
+        first_copy(to).start()
+
+    def others(act):
+        for k in range(pairs):
+            @pl.when(place(k, core) != tok)
+            def _():
+                act(place(k, core))
+
+    def own_sister():
+        return remote(x_in, rows_buf.at[tok], next_send.at[pair], x_recv.at[tok], seg, sister)
 
     @pl.when(seg == 0)
     def _():
-        for k in range(pairs):
-            first_copy(k).start()
+        others(first_start)
+        own_sister().start()
 
     spread = lax.broadcasted_iota(jnp.int32, (col_blocks, cols), 1) // blk
     spread = jnp.where(spread == lax.broadcasted_iota(jnp.int32, (col_blocks, cols), 0), 1.0, 0.0)
@@ -248,67 +267,86 @@
     acc[...] = jnp.zeros_like(acc)
     sq_sum[...] = jnp.zeros_like(sq_sum)
 
-    def relay(buf, k, src):
-        return remote(buf.at[src], buf.at[src], relay_send.at[k], x_recv.at[src], seg, sister)
-
-    def step(src):
-        x = x_buf[src].astype(f32)
+    def relay(buf, src):
+        return remote(buf.at[src], buf.at[src], relay_send.at[src // 2], x_recv.at[src], seg, sister)
+
+    def wide(src):
+        return gain[0:1, pl.ds(pl.multiple_of(src * cols, cols), cols)]
+
+    def square(x):
         sq = x * x
         part = sq[:, :LANES]
         for lo in range(LANES, cols, LANES):
             part = part + sq[:, lo:lo + LANES]
         sq_sum[...] += part
-        gained = (x * gain[0:1, pl.ds(pl.multiple_of(src * cols, cols), cols)]).astype(jnp.bfloat16)
-        acc[...] += jnp.dot(gained, w_buf[src], preferred_element_type=f32)
+
+    def row_scale():
+        mean_sq = jnp.sum(sq_sum[...], axis=1, keepdims=True) * (1.0 / width)
+        return lax.rsqrt(mean_sq + norm_eps)
+
+    def step(src):
+        x = x_buf[src].astype(f32)
+        square(x)
+        gained = x * wide(src)
+        high = gained.astype(jnp.bfloat16)
+        low = (gained - high.astype(f32)).astype(jnp.bfloat16)
+        both = jnp.dot(jnp.concatenate([high, low], axis=0), w_buf[src], preferred_element_type=f32)
+        acc[...] += both[:rows] + both[rows:]
+
+    gain_copy.wait()
 
     @pl.when(seg == 0)
     def _():
-        rows_buf[tok] = x_in[...]
-        for k in range(1, pairs):
-            src = place(pairs - k, core)
-            relay(rows_buf, k, src).wait_recv()
-            relay(rows_buf, k, src).start()
-        for k in range(pairs):
-            relay(rows_buf, k, place(pairs - k, 1 - core)).wait_recv()
+        def pass_on(src):
+            relay(rows_buf, src).wait_recv()
+            relay(rows_buf, src).start()
+
+        others(pass_on)
+        own_rows.wait()
+        for k in range(pairs):
+            relay(rows_buf, place(k, 1 - core)).wait_recv()
         for t in range(toks):
             for m in range(micro):
                 rows_f32[pl.ds((t * micro + m) * piece, piece), :] = rows_buf[t, m].astype(f32)
         for t in range(toks):
-            x_buf[t] = rows_f32[:, t * cols:(t + 1) * cols].astype(jnp.bfloat16)
+            x = rows_f32[:, t * cols:(t + 1) * cols]
+            square(x)
+            x_buf[t] = x.astype(jnp.bfloat16)
+        scale = row_scale()
 
         def one(src, carry):
+            normed = (x_buf[src].astype(f32) * scale * wide(src)).astype(jnp.bfloat16)
+            acc[...] += jnp.dot(normed, w_buf[src], preferred_element_type=f32)
+            return carry
+
+        lax.fori_loop(0, toks, one, 0)
+        others(lambda to: first_copy(to).wait_send())
+        own_sister().wait_send()
+        others(lambda src: relay(rows_buf, src).wait_send())
+
+    @pl.when(seg > 0)
+    def _():
+        def direct(k, carry):
+            src = place(k, core)
+            relay(x_buf, src).wait_recv()
+            relay(x_buf, src).start()
             step(src)
             return carry
 
-        lax.fori_loop(0, toks, one, 0)
-        for k in range(pairs):
-            first_copy(k).wait_send()
-        for k in range(1, pairs):
-            relay(rows_buf, k, place(pairs - k, core)).wait_send()
-
-    @pl.when(seg > 0)
-    def _():
-        def direct(k, carry):
-            src = place(k, core)
-            relay(x_buf, k, src).wait_recv()
-            relay(x_buf, k, src).start()
+        lax.fori_loop(0, pairs, direct, 0)
+
+        def relayed(k, carry):
+            src = place(k, 1 - core)
+            relay(x_buf, src).wait_recv()
             step(src)
             return carry
 
-        lax.fori_loop(0, pairs, direct, 0)
-
-        def relayed(k, carry):
-            src = place(k, 1 - core)
-            relay(x_buf, k, src).wait_recv()
-            step(src)
-            return carry
-
         lax.fori_loop(0, pairs, relayed, 0)
         for k in range(pairs):
-            relay(x_buf, k, place(k, core)).wait_send()
-
-    mean_sq = jnp.sum(sq_sum[...], axis=1, keepdims=True) * (1.0 / width)
-    y = x_buf[tok].astype(f32) + acc[...] * lax.rsqrt(mean_sq + norm_eps)
+            relay(x_buf, place(k, core)).wait_send()
+        acc[...] = acc[...] * row_scale()
+
+    y = x_buf[tok].astype(f32) + acc[...]
     y_send[...] = y.astype(jnp.bfloat16)
 
     def next_copy(k):
@@ -354,6 +392,7 @@
     nblk = keep_mask.shape[1]
     rows = micro * piece * toks
     vmem = pl.BlockSpec(memory_space=pltpu.VMEM)
+    hbm = pl.BlockSpec(memory_space=pltpu.HBM)
     bf16, f32 = jnp.bfloat16, jnp.float32
     dma = pltpu.SemaphoreType.DMA
     acts, group = pl.pallas_call(
@@ -362,9 +401,10 @@
             jax.ShapeDtypeStruct((1,) + inputs.shape, bf16),
             jax.ShapeDtypeStruct((rows, min(GRP, width)), bf16),
         ),
-        in_specs=[vmem, pl.BlockSpec(memory_space=pltpu.HBM), vmem, vmem],
+        in_specs=[hbm, hbm, vmem, hbm],
         out_specs=(vmem, vmem),
         scratch_shapes=[
+            pltpu.VMEM((1, width), f32),
             pltpu.VMEM((toks, width // toks, cols), bf16),
             pltpu.VMEM((toks, rows, cols), bf16),
             pltpu.VMEM((toks, micro, piece, width), bf16),
@@ -375,7 +415,7 @@
             pltpu.VMEM((rows, cols), bf16),
             pltpu.VMEM((toks, micro, piece, cols), bf16),
             pltpu.VMEM((toks, micro, piece, cols), bf16),
-            dma((toks,)), dma((toks,)), dma((toks,)), dma((toks,)), dma((toks,)), dma((toks,)),
+            dma((2,)), dma((toks,)), dma((toks,)), dma((toks,)), dma((toks,)), dma((toks,)), dma((toks,)),
         ],
         compiler_params=pltpu.CompilerParams(
             collective_id=0, has_side_effects=True, vmem_limit_bytes=48 * 2**20

time: 67.2 us -> 66.8 us (level)
  no operation moved by 1% of the time
where the time goes in v3:
time: 66.8 us; the launch traced here: 66.5 us
  Pallas kernels  62.9 us (94%)
  local copies, waits for them, and re-layouts  3 us (4%)
    pallas_call x1, Pallas kernels, local_kernel(): pl.pallas_call(forward_kernel, out_shape=(jax.ShapeDtypeStruct((1,) + inp...  54.1 us
    pallas_call x1, Pallas kernels, damped_factor(): pl.pallas_call(factor_kernel, out_shape=jax.ShapeDtypeStruct((size, size)...  8.81 us
    unnamed x6, local copies, waits for them, and re-layouts  3 us

profile of v3, /device:TPU:7, one launch (start us, length us, event | category | flops | bytes accessed | tf_op | source)
XLA Modules:
  0.0 66.5 jit_solution(5735529249855074054)
XLA Ops:
  0.6 0.8 %copy.6.keep = s32[1,64,8]{2,1,0:T(8,128)S(1)} copy(s32[1,64,8]{1,2,0:T(8,128)} %param.6) | data formatting | bytes 4096 | tf_op args[2]
  1.4 0.0 copy-start
  1.4 0.8 %copy-done = bf16[2,2,8192]{2,1,0:T(2,128)(2,1)S(1)} copy-done((bf16[2,2,8192]{2,1,0:T(2,128)(2,1)S(1)}, bf16[2,2,8192]{2,1,0:T(2,128)(2,1)}, u32[]{:S(2)}) %copy-start) | copy-done | bytes 65560
  2.2 0.0 copy-start.1
  2.2 0.8 %copy-done.1 = f32[1,8192]{1,0:T(1,128)S(1)} copy-done((f32[1,8192]{1,0:T(1,128)S(1)}, f32[1,8192]{1,0:T(1,128)}, u32[]{:S(2)}) %copy-start.1) | copy-done | bytes 32792
  3.0 54.1 %forward.1 = (bf16[1,2,2,8192]{3,2,1,0:T(2,128)(2,1)S(1)}, bf16[32,1024]{1,0:T(8,128)(2,1)S(1)}) custom-call(bf16[2,2,8192]{2,1,0:T(2,128)(2,1)S(1)} %copy-done, bf16[1,8192,1024]{2,1,0:T(8,128)(2,1)} %w_hbm.1, s32[1,64,8]{2,1,0:T(8,128)S(1)} %copy.6.keep, f32[1,8192]{1,0:T(1,128)S(1)} %copy-done.1), custom_call_target="tpu_custom_call" | custom-call | tf_op jit(solution)/shard_map/forward/pallas_call | solution.py:398
  57.1 8.8 %factor.1 = f32[1024,1024]{1,0:T(8,128)} custom-call(bf16[32,1024]{1,0:T(8,128)(2,1)S(1)} %get-tuple-element.5.x_ref), custom_call_target="tpu_custom_call" | custom-call | tf_op jit(solution)/shard_map/factor/pallas_call | solution.py:112
  65.9 0.6 copy.8
Async XLA Ops:
  1.4 0.8 %copy-start = (bf16[2,2,8192]{2,1,0:T(2,128)(2,1)S(1)}, bf16[2,2,8192]{2,1,0:T(2,128)(2,1)}, u32[]{:S(2)}) copy-start(bf16[2,2,8192]{2,1,0:T(2,128)(2,1)} %x_in.1) | copy-start | bytes 196612
  2.2 0.8 %copy-start.1 = (f32[1,8192]{1,0:T(1,128)S(1)}, f32[1,8192]{1,0:T(1,128)}, u32[]{:S(2)}) copy-start(f32[1,8192]{1,0:T(1,128)} %gain_hbm.1) | copy-start | bytes 98308
